TPU v7x, 256 devices: a whole 4x4x8 slice. The times are simulated.
256 devices in a mesh: dp: 8 (over x, core), code: 32 (over z, y).
Axes of the slice: x: 4, y: 4, z: 8, core: 2. Of those that a mesh axis runs over, the one named last changes fastest.
Arguments:
- latents: bfloat16 [4096, 256], P(('dp', 'code')), may hold values from -1000 to 1000
- out_grad: bfloat16 [4096, 256], P(('dp', 'code')), may hold values from -6 to 6
- targets: int32 [4096], P('dp'), may hold values from 0 to 262143
- codebook: bfloat16 [262144, 256], P('code'), may hold values from -2 to 2
Outputs:
- latent_grad: bfloat16 [4096, 256], P(('dp', 'code'))
- codebook_grad: float32 [262144, 256], P(('code', 'dp'))
- token_loss: float32 [4096], P(('dp', 'code'))
All inputs are finite; a program needn't handle non-finite values.
Results may differ from a plain program's by a relative error of at most 0.0042.
Values may be sent and summed in bfloat16 or wider, within the bound.
No kernel may reach another device: no remote copies, remote signals or barrier semaphores. Data moves between devices by JAX's collectives and lax.ppermute only.
A program may use at most 128 MiB of HBM per device.

v0:
```python
import jax
import jax.numpy as jnp
from jax import lax
from jax.sharding import PartitionSpec as P

ce_weight = 1.0


def per_device(latents, out_grad, targets, codebook):
    lat_all, grad_all = (
        lax.all_gather(latents, "code", axis=0, tiled=True),
        lax.all_gather(out_grad, "code", axis=0, tiled=True),
    )
    code_dev, feature_width = codebook.shape
    groups = lax.axis_size("dp")
    blocks = max(1, code_dev // 2048)
    sub_rows = code_dev // groups
    block_rows = sub_rows // blocks
    local_ids = targets - lax.axis_index("code") * code_dev
    layered = codebook.reshape(groups, blocks, block_rows, feature_width)
    dims_nt = (((1,), (1,)), ((), ()))

    def block_parts(block):
        book_block = layered[:, block].reshape(groups * block_rows, feature_width)
        code_ids = (
            jnp.arange(groups, dtype=jnp.int32)[:, None] * sub_rows
            + block * block_rows
            + jnp.arange(block_rows, dtype=jnp.int32)[None, :]
        ).reshape(-1)
        hit_mask = local_ids[:, None] == code_ids[None, :]
        logit_block = lax.dot_general(
            lat_all, book_block, dims_nt, preferred_element_type=jnp.float32
        )
        back_block = lax.dot_general(
            grad_all, book_block, dims_nt, preferred_element_type=jnp.float32
        )
        return (book_block, hit_mask, logit_block, back_block)

    tok_count = lat_all.shape[0]
    top = jnp.full((tok_count,), -jnp.inf, jnp.float32)
    total = jnp.zeros((tok_count,), jnp.float32)
    weighted = jnp.zeros((tok_count,), jnp.float32)
    picked = jnp.zeros((tok_count,), jnp.float32)
    for block in range(blocks):
        book_block, hit_mask, logit_block, back_block = block_parts(block)
        new_top = jnp.maximum(top, jnp.max(logit_block, axis=1))
        factor = jnp.exp(top - new_top)
        expo = jnp.exp(logit_block - new_top[:, None])
        total = total * factor + jnp.sum(expo, axis=1)
        weighted = weighted * factor + jnp.sum(expo * back_block, axis=1)
        picked = picked + jnp.sum(jnp.where(hit_mask, logit_block, 0.0), axis=1)
        top = new_top
    peak_value = lax.pmax(top, "code")
    rescale = jnp.exp(top - peak_value)
    total, weighted, picked = lax.psum((total * rescale, weighted * rescale, picked), "code")
    lse = peak_value + jnp.log(total)
    mean_back = weighted / total
    own_count = latents.shape[0]
    token_loss = lax.dynamic_slice_in_dim(
        lse - picked, lax.axis_index("code") * own_count, own_count, 0
    )
    valid = (local_ids >= 0) & (local_ids < code_dev)
    segment_ids = jnp.where(valid, local_ids, code_dev)
    direct = jax.ops.segment_sum(
        grad_all.astype(jnp.float32), segment_ids, num_segments=code_dev + 1
    )[:code_dev]
    direct = direct.reshape(groups, blocks, block_rows, feature_width)
    lat_grad = jnp.zeros((tok_count, feature_width), jnp.float32)
    collected = []
    for block in range(blocks):
        book_block, hit_mask, logit_block, back_block = block_parts(block)
        probs = jnp.exp(logit_block - lse[:, None])
        delta = probs * (back_block - mean_back[:, None]) + ce_weight * (
            probs - hit_mask.astype(jnp.float32)
        )
        delta = delta.astype(jnp.bfloat16)
        lat_grad = lat_grad + jnp.dot(delta, book_block, preferred_element_type=jnp.float32)
        term = lax.dot_general(
            delta, lat_all, (((0,), (0,)), ((), ())), preferred_element_type=jnp.float32
        )
        term = term + direct[:, block].reshape(groups * block_rows, feature_width)
        collected.append(term.reshape(groups, 1, block_rows, feature_width))
    whole = jnp.concatenate(collected, axis=1).reshape(code_dev, feature_width)
    codebook_grad = lax.psum_scatter(whole, "dp", scatter_dimension=0, tiled=True)
    latent_grad = lax.psum_scatter(lat_grad, "code", scatter_dimension=0, tiled=True).astype(
        jnp.bfloat16
    )
    return (latent_grad, codebook_grad, token_loss)


def solution(mesh):
    in_specs = (P(("dp", "code"), None), P(("dp", "code"), None), P("dp"), P("code", None))
    out_specs = (P(("dp", "code"), None), P(("code", "dp"), None), P(("dp", "code")))
    return jax.shard_map(
        per_device, mesh=mesh, in_specs=in_specs, out_specs=out_specs, check_vma=False
    )
```

profile of v0, /device:TPU:1, one launch (start us, length us, event | category | flops | bytes accessed | tf_op | source)
XLA Modules:
  0.0 585.0 jit_solution(4853329677700653990)
XLA Ops:
  7.2 0.0 reduce-scatter.3.cloned.1.call-start
  7.3 41.3 %all_gather.6 = bf16[512,256]{1,0:T(8,128)(2,1)S(1)} all-gather(bf16[16,256]{1,0:T(8,128)(2,1)} %param.4), channel_id=1, replica_groups=mesh['dp'=8,'code'=32] {'code'}, dimensions={0}, use_global_device_ids=true | all-gather | bytes 270336 | tf_op jit(solution)/shard_map/all_gather | solution.py:11
  48.6 36.1 %all_gather.7 = bf16[512,256]{1,0:T(8,128)(2,1)S(1)} all-gather(bf16[16,256]{1,0:T(8,128)(2,1)} %param.5), channel_id=1, replica_groups=mesh['dp'=8,'code'=32] {'code'}, dimensions={0}, use_global_device_ids=true | all-gather | bytes 270336 | tf_op jit(solution)/shard_map/all_gather | solution.py:12
  84.7 3.6 fusion.26
  88.2 2.7 fusion.33
  90.9 2.7 fusion.31
  93.6 2.7 fusion.28
  96.3 2.7 fusion.30
  99.0 2.7 fusion.32
  101.7 2.7 fusion.29
  104.4 0.1 add_bitcast_fusion.3
  104.5 0.1 add_bitcast_fusion
  104.6 0.1 add_bitcast_fusion.1
  104.7 0.1 add_bitcast_fusion.2
  104.8 2.7 fusion.27
  107.5 58.1 %pmax.7 = f32[512]{0:T(512)S(1)} all-reduce(f32[512]{0:T(512)S(1)} %get-tuple-element.22), channel_id=1, replica_groups=mesh['dp'=8,'code'=32] {'code'}, use_global_device_ids=true, to_apply=%region_4.5 | all-reduce | flops 512 | bytes 4096 | tf_op jit(solution)/shard_map/pmax | solution.py:53
  165.6 0.0 copy-done.10
  165.6 13.2 %fusion.18 = (f32[512]{0:T(512)S(1)}, f32[512]{0:T(512)S(1)}, f32[512]{0:T(512)S(1)}, f32[512]{0:T(512)S(1)}, f32[512]{0:T(512)S(1)}, /*index=5*/f32[512]{0:T(51...) fusion(f32[512,2048]{1,0:T(8,128)} %get-tuple-element.50, ...), kind=kOutput, calls=%fused_computation.36 | convolution fusion | flops 566224896 | bytes 34932736 | tf_op jit(solution)/shard_map/dot_general | solution.py:34
  178.8 57.1 %all-reduce = (f32[512]{0:T(512)S(1)}, f32[512]{0:T(512)S(1)}, f32[512]{0:T(512)S(1)}) all-reduce(f32[512]{0:T(512)S(1)} %get-tuple-element.34, f32[512]{0:T(512)S(1)} %get-tuple-element.33, f32[512]{0:T(512)S(1)} %add_add_fusion), channel_id=1, replica_groups=mesh['dp'=8,'code'=32] {'code'}, use_global_device_ids=true, to_apply=%region_14.15 | all-reduce | flops 1536 | bytes 12288 | tf_op jit(solution)/shard_map/psum | solution.py:55
  236.0 13.5 %fusion.16 = (bf16[512,2048]{1,0:T(8,128)(2,1)S(1)}, bf16[512,2048]{1,0:T(8,128)(2,1)S(1)}, bf16[512,2048]{1,0:T(8,128)(2,1)S(1)}, bf16[512,2048]{1,0:T(8,128)(2,1)S(1)}) fusion(f32[512,2048]{1,0:T(8,128)} %fusion.33, f32[512,2048]{1,0:T(8,128)} %get-tuple-element.52, s32[2048]{0:T(1024)S(1)} %bitcast.85, f32[512]{0:T(512)S(1)} %get-tuple-element.39, ...), kind=kLoop, calls=%fused_computation.26 | loop fusion | flops 33554432 | bytes 41981952 | tf_op jit(solution)/shard_map/convert_element_type | solution.py:76
  249.5 2.8 fusion.34
  252.4 1.9 convolution_add_fusion.6
  254.3 0.0 copy-done
  254.3 0.0 copy-done.4
  254.3 0.0 copy-done.2
  254.4 0.0 copy-done.7
  254.4 0.7 convolution_add_fusion.5
  255.1 1.5 convolution_add_fusion.4
  256.6 0.0 reduce-scatter.3.cloned.1.call-update
  256.7 0.0 reduce-scatter.5.cloned.1.call-start
  256.7 8.2 %scatter_custom_fusion = f32[8193,256]{1,0:T(8,128)} fusion(s32[512]{0:T(512)S(1)} %get-tuple-element.20, f32[]{:T(128)} %constant.11.clone.1, bf16[512,256]{1,0:T(8,128)(2,1)} %copy-done.9), kind=kCustom, calls=%fused_computation.10 | custom fusion | flops 262144 | bytes 8651780 | tf_op jit(solution)/shard_map/scatter-add | solution.py:64
  264.9 3.4 slice-done
  268.3 2.1 fusion.25
  270.4 0.0 copy-done.5
  270.4 2.5 convolution_add_fusion.2
  273.0 0.0 copy-done.3
  273.0 0.0 copy-start.1
  273.0 0.8 convolution_add_fusion.1
  273.7 0.8 copy-done.1
  274.6 0.7 convolution_add_fusion.3
  275.3 0.8 convolution_add_fusion
  276.1 0.8 pad_maximum_fusion
  276.9 3.8 copy.8
  280.7 0.0 reduce-scatter.5.cloned.1.call-update
  280.8 0.6 dynamic_slice.3
  281.3 235.7 %reduce-scatter.3.cloned.1.call-done = f32[16,256]{1,0:T(8,128)} async-done(((f32[512,256]{1,0:T(8,128)}), f32[16,256]{1,0:T(8,128)}) %reduce-scatter.3.cloned.1.call-update) | async-done | bytes 16400 | tf_op jit(solution)/shard_map/reduce_scatter | solution.py:85
  517.0 1.3 convert_element_type.38
  518.4 59.8 %reduce-scatter.5.cloned.1.call-done = f32[1024,256]{1,0:T(8,128)} async-done(((f32[8192,256]{1,0:T(8,128)}), f32[1024,256]{1,0:T(8,128)}) %reduce-scatter.5.cloned.1.call-update) | async-done | bytes 1048592 | tf_op jit(solution)/shard_map/reduce_scatter | solution.py:84
  (31 shorter events, 0.1 us)
Async XLA Ops:
  7.2 509.9 %reduce-scatter.3.cloned.1.call-start = ((), (), s32[]{:S(2)}) async-start(), calls=%async_computation.2 | async-start | bytes 540672 | tf_op jit(solution)/shard_map/reduce_scatter | solution.py:85
  84.7 14.3 %copy-start.9 = (bf16[512,256]{1,0:T(8,128)(2,1)}, bf16[512,256]{1,0:T(8,128)(2,1)S(1)}, u32[]{:S(2)}) copy-start(bf16[512,256]{1,0:T(8,128)(2,1)S(1)} %all_gather.7) | copy-start | bytes 786436
  88.2 8.1 %copy-start.8 = (bf16[8,1,256,256]{3,2,1,0:T(8,128)(2,1)}, bf16[8,1,256,256]{3,2,1,0:T(8,128)(2,1)S(1)}, u32[]{:S(2)}) copy-start(bf16[8,1,256,256]{3,2,1,0:T(8,128)(2,1)S(1)} %get-tuple-element.29) | copy-start | bytes 3145732
  88.2 13.5 %copy-start.6 = (bf16[8,1,256,256]{3,2,1,0:T(8,128)(2,1)}, bf16[8,1,256,256]{3,2,1,0:T(8,128)(2,1)S(1)}, u32[]{:S(2)}) copy-start(bf16[8,1,256,256]{3,2,1,0:T(8,128)(2,1)S(1)} %get-tuple-element.31) | copy-start | bytes 3145732
  99.0 5.7 copy-start.11
  104.4 61.2 %copy-start.12 = (s32[512]{0:T(512)S(1)}, s32[512]{0:T(512)}, u32[]{:S(2)}) copy-start(s32[512]{0:T(512)} %param.6) | copy-start | bytes 6148
  104.4 61.2 %copy-start.10 = (bf16[512,256]{1,0:T(8,128)(2,1)S(1)}, bf16[512,256]{1,0:T(8,128)(2,1)}, u32[]{:S(2)}) copy-start(bf16[512,256]{1,0:T(8,128)(2,1)} %copy-done.9) | copy-start | bytes 786436
  249.5 4.8 copy-start
  249.5 4.8 copy-start.4
  249.5 4.8 copy-start.2
  249.5 4.8 copy-start.7
  256.7 321.5 %reduce-scatter.5.cloned.1.call-start = ((), (), s32[]{:S(2)}) async-start(), calls=%async_computation.3 | async-start | bytes 9437184 | tf_op jit(solution)/shard_map/reduce_scatter | solution.py:84
  264.9 3.4 slice-start
  268.3 2.1 copy-start.5
  270.4 2.5 copy-start.3
  273.0 1.6 copy-start.1
Sparse Core Ops, SparseCore 0:
  256.8 260.2 reduce-scatter.2
  520.2 57.9 reduce-scatter.4
where the time goes:
time: 585 us
  waiting for transfers between devices  296 us (51%)
  blocking collectives  193 us (33%)
  matrix products  43.9 us (8%)
  other arithmetic  24.2 us (4%)
  local copies, waits for them, and re-layouts  14.4 us (2%)
  between operations  14.3 us (2%)
    reduce_scatter x1, waiting for transfers between devices, per_device(): lax.psum_scatter(lat_grad, 'code', scatter_dimension=0, tiled=True)  236 us
    reduce_scatter x1, waiting for transfers between devices, per_device(): lax.psum_scatter(whole, 'dp', scatter_dimension=0, tiled=True)  59.8 us
    pmax x1, blocking collectives, per_device(): peak_value = lax.pmax(top, 'code')  58.1 us
    psum x1, blocking collectives, per_device(): lax.psum((total * rescale, weighted * rescale, picked), 'code')  57.1 us
    all_gather x1, blocking collectives, per_device(): lax.all_gather(latents, 'code', axis=0, tiled=True)  41.3 us
    all_gather x1, blocking collectives, per_device(): lax.all_gather(out_grad, 'code', axis=0, tiled=True)  36.1 us
    dot_general x4, matrix products, block_parts(): lax.dot_general(grad_all, book_block, dims_nt, preferred_element_type=jnp...  21.3 us
    convert_element_type x1, other arithmetic, per_device(): delta = delta.astype(jnp.bfloat16)  13.5 us
  transfers between devices with their start and end apart: 2, of which 2 were waited for; matrix products, arithmetic and copies ran while one was open for 4% of the time, Pallas kernels for 0%

commit v1 on v0

--- a/solution.py
+++ b/solution.py
@@ -8,7 +8,15 @@
 
 def per_device(latents, out_grad, targets, codebook):
     lat_all, grad_all = (
-        lax.all_gather(latents, "code", axis=0, tiled=True),
+        jnp.concatenate(
+            lax.all_to_all(
+                jnp.stack([latents for _ in range(lax.axis_size("code"))]),
+                axis_name="code",
+                split_axis=0,
+                concat_axis=0,
+            ),
+            0,
+        ),
         lax.all_gather(out_grad, "code", axis=0, tiled=True),
     )
     code_dev, feature_width = codebook.shape

time: 585 us -> 565 us (0.966)
  blocking collectives: 193 us -> 154 us
  starting transfers between devices: 0.08 us -> 12.1 us
    all_gather x1 -> x0, blocking collectives: 41.3 us -> none  [per_device(): lax.all_gather(latents, 'code', axis=0, tiled=True)]
    all_to_all x0 -> x1, starting transfers between devices: none -> 12 us  [per_device(): lax.all_to_all(jnp.stack([latents for _ in range(lax.axis_size('code'))])...]
  transfers between devices with their start and end apart: 2 -> 3, of which waited for: 2 -> 2; matrix products, arithmetic and copies ran while one was open for 4% -> 6% of each run, Pallas kernels for 0% -> 0%
where the time goes in v1:
time: 565 us; the launch traced here: 564 us
  waiting for transfers between devices  296 us (52%)
  blocking collectives  154 us (27%)
  matrix products  44.5 us (8%)
  other arithmetic  24.2 us (4%)
  local copies, waits for them, and re-layouts  18.8 us (3%)
  between operations  14.3 us (3%)
  starting transfers between devices  12.1 us (2%)
    reduce_scatter x1, waiting for transfers between devices, per_device(): lax.psum_scatter(lat_grad, 'code', scatter_dimension=0, tiled=True)  236 us
    reduce_scatter x1, waiting for transfers between devices, per_device(): lax.psum_scatter(whole, 'dp', scatter_dimension=0, tiled=True)  59.9 us
    pmax x1, blocking collectives, per_device(): peak_value = lax.pmax(top, 'code')  58.4 us
    psum x1, blocking collectives, per_device(): lax.psum((total * rescale, weighted * rescale, picked), 'code')  56.7 us
    all_gather x1, blocking collectives, per_device(): lax.all_gather(out_grad, 'code', axis=0, tiled=True)  39.1 us
    dot_general x4, matrix products, block_parts(): lax.dot_general(grad_all, book_block, dims_nt, preferred_element_type=jnp...  21.2 us
    convert_element_type x1, other arithmetic, per_device(): delta = delta.astype(jnp.bfloat16)  13.5 us
    all_to_all x1, starting transfers between devices, per_device(): lax.all_to_all(jnp.stack([latents for _ in range(lax.axis_size('code'))])...  12 us
  transfers between devices with their start and end apart: 3, of which 2 were waited for; matrix products, arithmetic and copies ran while one was open for 6% of the time, Pallas kernels for 0%

profile of v1, /device:TPU:1, one launch (start us, length us, event | category | flops | bytes accessed | tf_op | source)
XLA Modules:
  0.0 564.1 jit_solution(1819957416965113240)
XLA Ops:
  7.2 1.4 stack.2
  8.6 12.0 %all-to-all-start = ((bf16[32,16,256]{2,1,0:T(8,128)(2,1)}), bf16[32,16,256]{2,1,0:T(8,128)(2,1)S(1)}, u32[]{:S(2)}, u32[]{:S(2)}) async-start(bf16[32,16,256]{2,1,0:T(8,128)(2,1)} %stack.2), calls=%async_computation | async-start | bytes 524288 | tf_op jit(solution)/shard_map/all_to_all | solution.py:12
  20.6 0.0 reduce-scatter.3.cloned.1.call-start
  20.7 0.1 add_bitcast_fusion.3
  20.8 0.1 add_bitcast_fusion
  20.9 0.1 add_bitcast_fusion.1
  20.9 0.1 add_bitcast_fusion.2
  21.0 39.1 %all_gather.3 = bf16[512,256]{1,0:T(8,128)(2,1)S(1)} all-gather(bf16[16,256]{1,0:T(8,128)(2,1)} %param.5), channel_id=1, replica_groups=mesh['dp'=8,'code'=32] {'code'}, dimensions={0}, use_global_device_ids=true | all-gather | bytes 270336 | tf_op jit(solution)/shard_map/all_gather | solution.py:20
  60.1 3.6 fusion.26
  63.7 2.7 fusion.33
  66.4 2.7 fusion.31
  69.1 2.7 fusion.32
  71.8 0.0 copy-done.15
  71.8 8.2 %scatter_custom_fusion = f32[8193,256]{1,0:T(8,128)} fusion(s32[512]{0:T(512)S(1)} %get-tuple-element.20, f32[]{:T(128)} %constant.11.clone.1, bf16[512,256]{1,0:T(8,128)(2,1)} %copy-done.11), kind=kCustom, calls=%fused_computation.10 | custom fusion | flops 262144 | bytes 8651780 | tf_op jit(solution)/shard_map/scatter-add | solution.py:72
  80.0 3.4 slice-done
  83.4 3.3 fusion.25
  86.7 0.0 all-to-all-done
  86.7 2.7 fusion.28
  89.4 2.7 fusion.30
  92.1 2.7 fusion.29
  94.8 0.0 copy-done.13
  94.8 2.7 fusion.27
  97.6 58.4 %pmax.7 = f32[512]{0:T(512)S(1)} all-reduce(f32[512]{0:T(512)S(1)} %get-tuple-element.22), channel_id=1, replica_groups=mesh['dp'=8,'code'=32] {'code'}, use_global_device_ids=true, to_apply=%region_4.5 | all-reduce | flops 512 | bytes 4096 | tf_op jit(solution)/shard_map/pmax | solution.py:61
  156.0 13.1 %fusion.18 = (f32[512]{0:T(512)S(1)}, f32[512]{0:T(512)S(1)}, f32[512]{0:T(512)S(1)}, f32[512]{0:T(512)S(1)}, f32[512]{0:T(512)S(1)}, /*index=5*/f32[512]{0:T(51...) fusion(f32[512,2048]{1,0:T(8,128)} %get-tuple-element.50, ...), kind=kOutput, calls=%fused_computation.36 | convolution fusion | flops 566224896 | bytes 34932736 | tf_op jit(solution)/shard_map/dot_general | solution.py:42
  169.2 56.7 %all-reduce = (f32[512]{0:T(512)S(1)}, f32[512]{0:T(512)S(1)}, f32[512]{0:T(512)S(1)}) all-reduce(f32[512]{0:T(512)S(1)} %get-tuple-element.34, f32[512]{0:T(512)S(1)} %get-tuple-element.33, f32[512]{0:T(512)S(1)} %add_add_fusion), channel_id=1, replica_groups=mesh['dp'=8,'code'=32] {'code'}, use_global_device_ids=true, to_apply=%region_14.15 | all-reduce | flops 1536 | bytes 12288 | tf_op jit(solution)/shard_map/psum | solution.py:63
  225.9 13.5 %fusion.16 = (bf16[512,2048]{1,0:T(8,128)(2,1)S(1)}, bf16[512,2048]{1,0:T(8,128)(2,1)S(1)}, bf16[512,2048]{1,0:T(8,128)(2,1)S(1)}, bf16[512,2048]{1,0:T(8,128)(2,1)S(1)}) fusion(f32[512,2048]{1,0:T(8,128)} %fusion.33, f32[512,2048]{1,0:T(8,128)} %get-tuple-element.52, s32[2048]{0:T(1024)S(1)} %bitcast.94, f32[512]{0:T(512)S(1)} %get-tuple-element.39, ...), kind=kLoop, calls=%fused_computation.26 | loop fusion | flops 33554432 | bytes 41981952 | tf_op jit(solution)/shard_map/convert_element_type | solution.py:84
  239.4 0.0 copy-start
  239.5 2.8 fusion.34
  242.3 1.9 convolution_add_fusion.6
  244.3 0.7 convolution_add_fusion.5
  245.0 1.6 convolution_add_fusion.4
  246.6 0.0 reduce-scatter.3.cloned.1.call-update
  246.6 0.0 reduce-scatter.5.cloned.1.call-start
  246.7 3.1 convolution_add_fusion.2
  249.8 0.3 copy-done.7
  250.2 0.8 convolution_add_fusion.1
  250.9 0.8 copy-done.1
  251.7 0.6 copy-done.6
  252.4 0.7 convolution_add_fusion.3
  253.1 0.8 copy-done.5
  254.0 0.8 convolution_add_fusion
  254.7 0.8 pad_maximum_fusion
  255.6 3.8 copy.8
  259.4 0.0 reduce-scatter.5.cloned.1.call-update
  259.4 0.6 dynamic_slice.3
  260.0 236.1 %reduce-scatter.3.cloned.1.call-done = f32[16,256]{1,0:T(8,128)} async-done(((f32[512,256]{1,0:T(8,128)}), f32[16,256]{1,0:T(8,128)}) %reduce-scatter.3.cloned.1.call-update) | async-done | bytes 16400 | tf_op jit(solution)/shard_map/reduce_scatter | solution.py:93
  496.1 1.3 convert_element_type.38
  497.4 59.9 %reduce-scatter.5.cloned.1.call-done = f32[1024,256]{1,0:T(8,128)} async-done(((f32[8192,256]{1,0:T(8,128)}), f32[1024,256]{1,0:T(8,128)}) %reduce-scatter.5.cloned.1.call-update) | async-done | bytes 1048592 | tf_op jit(solution)/shard_map/reduce_scatter | solution.py:92
  (39 shorter events, 0.1 us)
Async XLA Ops:
  8.6 78.1 %all-to-all-start = ((bf16[32,16,256]{2,1,0:T(8,128)(2,1)}), bf16[32,16,256]{2,1,0:T(8,128)(2,1)S(1)}, u32[]{:S(2)}, u32[]{:S(2)}) async-start(bf16[32,16,256]{2,1,0:T(8,128)(2,1)} %stack.2), calls=%async_computation | async-start | bytes 524288 | tf_op jit(solution)/shard_map/all_to_all | solution.py:12
  20.6 475.4 %reduce-scatter.3.cloned.1.call-start = ((), (), s32[]{:S(2)}) async-start(), calls=%async_computation.3 | async-start | bytes 540672 | tf_op jit(solution)/shard_map/reduce_scatter | solution.py:93
  60.1 9.0 %copy-start.11 = (bf16[512,256]{1,0:T(8,128)(2,1)}, bf16[512,256]{1,0:T(8,128)(2,1)S(1)}, u32[]{:S(2)}) copy-start(bf16[512,256]{1,0:T(8,128)(2,1)S(1)} %all_gather.3) | copy-start | bytes 786436
  63.7 25.7 %copy-start.10 = (bf16[8,1,256,256]{3,2,1,0:T(8,128)(2,1)}, bf16[8,1,256,256]{3,2,1,0:T(8,128)(2,1)S(1)}, u32[]{:S(2)}) copy-start(bf16[8,1,256,256]{3,2,1,0:T(8,128)(2,1)S(1)} %get-tuple-element.29) | copy-start | bytes 3145732
  63.7 28.5 %copy-start.8 = (bf16[8,1,256,256]{3,2,1,0:T(8,128)(2,1)}, bf16[8,1,256,256]{3,2,1,0:T(8,128)(2,1)S(1)}, u32[]{:S(2)}) copy-start(bf16[8,1,256,256]{3,2,1,0:T(8,128)(2,1)S(1)} %get-tuple-element.31) | copy-start | bytes 3145732
  66.4 5.4 copy-start.15
  80.0 3.4 slice-start
  89.4 5.4 copy-start.13
  92.1 63.8 %copy-start.12 = (bf16[512,256]{1,0:T(8,128)(2,1)S(1)}, bf16[512,256]{1,0:T(8,128)(2,1)}, u32[]{:S(2)}) copy-start(bf16[512,256]{1,0:T(8,128)(2,1)} %copy-done.11) | copy-start | bytes 786436
  94.8 61.1 %copy-start.14 = (bf16[8,1,256,256]{3,2,1,0:T(8,128)(2,1)S(1)}, bf16[8,1,256,256]{3,2,1,0:T(8,128)(2,1)}, u32[]{:S(2)}) copy-start(bf16[8,1,256,256]{3,2,1,0:T(8,128)(2,1)} %get-tuple-element.32) | copy-start | bytes 3145732
  239.4 4.8 copy-start
  239.4 4.8 copy-start.4
  239.4 4.8 copy-start.2
  239.5 4.8 copy-start.9
  246.6 310.7 %reduce-scatter.5.cloned.1.call-start = ((), (), s32[]{:S(2)}) async-start(), calls=%async_computation.4 | async-start | bytes 9437184 | tf_op jit(solution)/shard_map/reduce_scatter | solution.py:92
  246.7 3.1 copy-start.3
  246.7 3.5 copy-start.7
  250.1 1.6 copy-start.1
  250.1 2.2 copy-start.6
  252.4 1.6 copy-start.5
Sparse Core Ops, SparseCore 0:
  246.7 249.2 reduce-scatter.2
  499.2 58.0 reduce-scatter.4
